TPU v7x, 32 devices: a whole 2x2x4 slice. The times are simulated.
32 devices in a mesh: section: 2 (over x), dp: 4 (over z), mp: 4 (over y, core).
Axes of the slice: x: 2, y: 2, z: 4, core: 2. Of those that a mesh axis runs over, the one named last changes fastest.
Arguments:
- hidden: bfloat16 [2, 512, 4096], P('section', 'dp'), may hold values from -9 to 9
- norm_gain: float32 [2, 4096], P('section'), may hold values from 0.5 to 1.5
- kv_weight: bfloat16 [2, 4096, 2048], P('section', None, 'mp'), may hold values from -1 to 1
- attn_flat: bfloat16 [2, 4, 8388608], P('section', 'mp', 'dp'), may hold values from -1 to 1
- final_gain: float32 [4096], replicated, may hold values from 0.5 to 1.5
- reward_head: float32 [4096], replicated, may hold values from -0.09375 to 0.09375
- segment_ids: int32 [2, 4], P('section'), may hold values from 0 to 2, never falling along the last dimension, each value on 1 to 2 neighbouring positions
- ranks: int32 [2], replicated, may hold values from 0 to 999
Outputs:
- next_hidden: bfloat16 [2, 512, 4096], P('section', 'dp')
- rewards: float32 [2], replicated
- pair_loss: float32 [2, 2], replicated
Inputs may be any that keep to these rules, and one draw needn't show every extreme that they name: `segment_ids`: each row's segment numbers never fall, every number of 0 to 2 is present, each on 1 to 2 blocks, one on exactly 2.
All inputs are finite; a program needn't handle non-finite values.
Results may differ from a plain program's by a relative error of at most 0.035.
Values may be sent and summed in bfloat16 or wider, within the bound.
A program may use at most 128 MiB of HBM per device.

v0:
```python
import jax
import jax.numpy as jnp
from jax import lax
from jax.sharding import PartitionSpec as P

HD = 128
QH = 32
KVH = 8
EPS = 1e-05


def passed_along(block, axis, distance):
    devices = range(lax.axis_size(axis))
    route = [(i - distance, i) for i in devices if i - distance in devices]
    return lax.ppermute(block, axis, route)


def shards(hidden, norm_gain, kv_weight, attn_flat, final_gain, reward_head, segment_ids, ranks):
    state = hidden[0]
    tokens = state.shape[0]
    width = state.shape[1]
    seg_row = segment_ids[0]
    blocks = lax.axis_size("dp")
    block = lax.axis_index("dp")
    phases = lax.axis_size("section")
    phase_now = lax.axis_index("section")
    responses = ranks.shape[0]
    state_wide = state.astype(jnp.float32)
    normed = (
        state_wide
        * lax.rsqrt(jnp.mean(state_wide * state_wide, -1, keepdims=True) + EPS)
        * norm_gain[0]
    ).astype(jnp.bfloat16)
    keyval = jnp.dot(normed, kv_weight[0], preferred_element_type=jnp.float32).astype(jnp.bfloat16)
    kv_local = keyval.shape[1] // (2 * HD)
    group = QH // KVH
    q_width = kv_local * group * HD
    flat = lax.all_gather(attn_flat[0, 0], "dp", axis=0, tiled=True)
    w_query = flat[: width * q_width].reshape(width, q_width)
    w_out = flat[width * q_width : 2 * width * q_width].reshape(q_width, width)
    query = jnp.dot(normed, w_query, preferred_element_type=jnp.float32).astype(jnp.bfloat16)
    query = query.reshape(tokens, kv_local, group, HD)
    block_ids = jnp.arange(blocks, dtype=jnp.int32)
    own_seg = jnp.sum(jnp.where(block_ids == block, seg_row, 0))
    query_pos = block * tokens + jnp.arange(tokens, dtype=jnp.int32)
    piece = lax.all_gather(keyval, "dp", axis=0, tiled=True)
    peak = jnp.full((kv_local, group, tokens), -1e30, jnp.float32)
    count = piece.shape[0]
    key_pos = jnp.arange(count, dtype=jnp.int32)
    key_block = key_pos // tokens
    key_seg = jnp.sum(jnp.where(key_block[:, None] == block_ids[None, :], seg_row[None, :], 0), 1)
    parts = piece.reshape(count, kv_local, 2, HD)
    keys = parts[:, :, 0]
    values = parts[:, :, 1]
    earlier = (key_block < block) & (key_block >= 0) & ((key_seg == 0) | (key_seg == own_seg))
    same = (key_block == block)[None, :] & (key_pos[None, :] <= query_pos[:, None])
    visible = earlier[None, :] | same
    scores = jnp.einsum("tjgd,cjd->jgtc", query, keys, preferred_element_type=jnp.float32) * HD ** (
        -0.5
    )
    scores = jnp.where(visible[None, None], scores, -1e30)
    new_peak = jnp.maximum(peak, jnp.max(scores, -1))
    weights = jnp.where(visible[None, None], jnp.exp(scores - new_peak[..., None]), 0.0)
    total = jnp.sum(weights, -1)
    accum = jnp.einsum(
        "jgtc,cjd->jgtd", weights.astype(jnp.bfloat16), values, preferred_element_type=jnp.float32
    )
    peak, total, accum = (new_peak, total, accum)
    mixed = (
        (accum / total[..., None])
        .transpose(2, 0, 1, 3)
        .reshape(tokens, q_width)
        .astype(jnp.bfloat16)
    )
    partial_value = jnp.dot(mixed, w_out, preferred_element_type=jnp.float32)
    ends = (
        jnp.sum(
            (seg_row[None, :] <= jnp.arange(1, responses + 1, dtype=jnp.int32)[:, None]).astype(
                jnp.int32
            ),
            1,
        )
        - 1
    )
    at_end = (ends == block) & (phase_now == phases - 1)
    summed = lax.psum(partial_value.astype(jnp.bfloat16), "mp").astype(jnp.float32)
    updated = (state_wide + summed).astype(jnp.bfloat16)
    moved = passed_along(updated, "section", 1)
    last_row = updated[tokens - 1].astype(jnp.float32)
    squares = jnp.sum(last_row * last_row)
    product = jnp.sum(last_row * final_gain * reward_head)
    sums_sq, dots = lax.psum(
        (jnp.where(at_end, squares, 0.0), jnp.where(at_end, product, 0.0)), ("section", "dp")
    )
    rewards = dots * lax.rsqrt(sums_sq / width + EPS)
    pair_loss = jnp.where(
        ranks[:, None] < ranks[None, :], jax.nn.softplus(rewards[None, :] - rewards[:, None]), 0.0
    )
    return (moved[None], rewards, pair_loss)


def solution(mesh):
    placed = (
        P("section", "dp", None),
        P("section", None),
        P("section", None, "mp"),
        P("section", "mp", "dp"),
        P(),
        P(),
        P("section", None),
        P(),
    )
    return jax.shard_map(
        shards,
        mesh=mesh,
        in_specs=placed,
        out_specs=(P("section", "dp", None), P(), P()),
        check_vma=False,
    )
```

profile of v0, /device:TPU:0, one launch (start us, length us, event | category | flops | bytes accessed | tf_op | source)
XLA Modules:
  0.0 864.1 jit_solution(7415746184136145379)
XLA Ops:
  7.2 0.0 copy-start.1
  7.2 0.0 copy-start.7
  7.2 0.0 all-gather.3.cloned.1.call-start
  7.2 0.7 all-gather.3.cloned.1.call-update
  7.9 0.0 all-reduce.3.cloned.1.call-start
  8.0 0.4 copy-done.1
  8.4 0.3 fusion.5
  8.7 0.0 copy-done.7
  8.7 2.9 fusion.16
  11.6 17.4 %all_gather.6 = bf16[512,512]{1,0:T(8,128)(2,1)S(1)} all-gather(bf16[128,512]{1,0:T(8,128)(2,1)S(1)} %fusion.16), channel_id=1, replica_groups=mesh['section'=2,'dp'=4,'mp'=4] {'dp'}, dimensions={0}, use_global_device_ids=true | all-gather | bytes 655360 | tf_op jit(solution)/shard_map/all_gather | solution.py:46
  29.0 0.0 copy-start.6
  29.0 0.1 reshape.161
  29.1 0.7 fusion.48
  29.9 0.7 copy.22
  30.6 0.0 copy-done.6
  30.6 0.6 fusion.44
  31.2 0.1 select_reduce_fusion
  31.3 0.7 or_and_fusion
  32.0 0.2 fusion.35
  32.2 541.5 %all-gather.3.cloned.1.call-done = bf16[1,1,8388608]{2,1,0:T(2,128)(2,1)} async-done(((bf16[1,1,2097152]{2,1,0:T(2,128)(2,1)}), bf16[1,1,8388608]{2,1,0:T(2,128)(2,1)}) %all-gather.3.cloned.1.call-update) | async-done | bytes 16777232 | tf_op jit(solution)/shard_map/all_gather | solution.py:38
  573.7 183.8 %slice_reduce_fusion = (bf16[4194304]{0:T(1024)(128)(2,1)}, bf16[4194304]{0:T(1024)(128)(2,1)}) fusion(bf16[1,1,8388608]{2,1,0:T(2,128)(2,1)} %all-gather.3.cloned.1.call-done), kind=kLoop, calls=%fused_computation | loop fusion | bytes 33554432 | tf_op jit(solution)/shard_map/slice | solution.py:40
  757.6 13.3 %slice.40 = bf16[1024,4096]{1,0:T(8,128)(2,1)} reshape(bf16[4194304]{0:T(1024)(128)(2,1)} %get-tuple-element.3) | data formatting | bytes 16777216 | tf_op jit(solution)/shard_map/slice | solution.py:40
  770.9 13.3 %slice.37 = bf16[4096,1024]{1,0:T(8,128)(2,1)} reshape(bf16[4194304]{0:T(1024)(128)(2,1)} %get-tuple-element.4) | data formatting | bytes 16777216 | tf_op jit(solution)/shard_map/slice | solution.py:39
  784.2 4.7 convolution_convert_fusion.1
  788.9 0.2 reshape.162
  789.0 0.0 copy-start
  789.0 0.5 fusion.11
  789.5 0.5 fusion.12
  790.1 0.7 fusion.15
  790.7 1.7 copy-done
  792.4 2.3 convolution_convert_fusion
  794.7 0.0 copy-start.2
  794.7 0.0 copy-start.3
  794.7 0.0 all-reduce.3.cloned.1.call-update
  794.7 0.2 fusion.43
  794.9 34.2 %all-reduce.3.cloned.1.call-done = bf16[128,4096]{1,0:T(8,128)(2,1)} async-done(((bf16[128,4096]{1,0:T(8,128)(2,1)}), bf16[128,4096]{1,0:T(8,128)(2,1)}) %all-reduce.3.cloned.1.call-update) | async-done | bytes 1048592 | tf_op jit(solution)/shard_map/psum | solution.py:86
  829.1 1.5 fusion.8
  830.6 3.4 collective-permute-start
  834.1 0.0 copy-done.2
  834.1 0.0 copy-done.3
  834.1 0.6 multiply_reduce_fusion
  834.7 1.3 broadcast_select_fusion
  836.0 19.5 %all-reduce = (f32[2]{0:T(128)S(1)}, f32[2]{0:T(128)S(1)}) all-reduce(f32[2]{0:T(128)S(1)} %get-tuple-element.12, f32[2]{0:T(128)S(1)} %get-tuple-element.11), channel_id=1, replica_groups=mesh['section'=2,'dp'=4,'mp'=4] {'section','dp'}, use_global_device_ids=true, to_apply=%region_8.9 | all-reduce | flops 4 | bytes 32 | tf_op jit(solution)/shard_map/psum | solution.py:92
  855.5 0.0 copy-done.4
  855.5 0.7 compare_select_fusion.1
  856.2 0.1 collective-permute-done
  856.3 1.0 copy.34
  857.3 0.0 copy-done.5
  (9 shorter events, 0.1 us)
Async XLA Ops:
  7.2 1.2 copy-start.1
  7.2 1.5 copy-start.7
  7.2 566.5 %all-gather.3.cloned.1.call-start = ((), (), s32[]{:S(2)}) async-start(), calls=%async_computation.1 | async-start | bytes 41943040 | tf_op jit(solution)/shard_map/all_gather | solution.py:38
  7.9 821.2 %all-reduce.3.cloned.1.call-start = ((), (), s32[]{:S(2)}) async-start(), calls=%async_computation | async-start | bytes 2097152 | tf_op jit(solution)/shard_map/psum | solution.py:86
  29.0 1.6 copy-start.6
  789.0 3.4 copy-start
  794.7 39.4 %copy-start.2 = (f32[4096]{0:T(1024)S(1)}, f32[4096]{0:T(1024)}, u32[]{:S(2)}) copy-start(f32[4096]{0:T(1024)} %param.13) | copy-start | bytes 49156
  794.7 39.4 %copy-start.3 = (f32[4096]{0:T(1024)S(1)}, f32[4096]{0:T(1024)}, u32[]{:S(2)}) copy-start(f32[4096]{0:T(1024)} %param.12) | copy-start | bytes 49156
  794.7 60.9 %copy-start.4 = (s32[2]{0:T(128)S(1)}, s32[2]{0:T(128)}, u32[]{:S(2)}) copy-start(s32[2]{0:T(128)} %param.15) | copy-start | bytes 28
  830.6 25.7 %collective-permute-start = (bf16[128,4096]{1,0:T(8,128)(2,1)S(1)}, bf16[128,4096]{1,0:T(8,128)(2,1)S(1)}, u32[]{:S(2)}, u32[]{:S(2)}) collective-permute-start(bf16[128,4096]{1,0:T(8,128)(2,1)S(1)} %fusion.8), channel_id=1, source_target_pairs={{0,16},{1,17},{2,18},{3,19},{4,20},{5,21},{6,22},{7,23},{8,24},{9,... | collective-permute-start | bytes 3145736 | tf_op jit(solution)/shard_map/ppermute | solution.py:15
  855.5 1.8 copy-start.5
Sparse Core Ops, SparseCore 0:
  9.6 564.0 all-gather.2
  794.8 34.2 all-reduce.2
where the time goes:
time: 865 us; the launch traced here: 864 us
  waiting for transfers between devices  577 us (67%)
  local copies, waits for them, and re-layouts  215 us (25%)
  blocking collectives  36.9 us (4%)
  between operations  14.3 us (2%)
  matrix products  11 us (1%)
    all_gather x1, waiting for transfers between devices, shards(): flat = lax.all_gather(attn_flat[0, 0], 'dp', axis=0, tiled=True)  542 us
    slice x2, local copies, waits for them, and re-layouts, shards(): w_out = flat[width * q_width:2 * width * q_width].reshape(q_width, width)  197 us
    psum x1, waiting for transfers between devices, shards(): lax.psum(partial_value.astype(jnp.bfloat16), 'mp').astype(jnp.float32)  34.2 us
    psum x1, blocking collectives, shards(): lax.psum((jnp.where(at_end, squares, 0.0), jnp.where(at_end, product, 0.0...  19.5 us
    all_gather x1, blocking collectives, shards(): piece = lax.all_gather(keyval, 'dp', axis=0, tiled=True)  17.4 us
  transfers between devices with their start and end apart: 3, of which 3 were waited for; matrix products, arithmetic and copies ran while one was open for 1% of the time, Pallas kernels for 0%

commit v1 on v0

--- a/solution.py
+++ b/solution.py
@@ -7,6 +7,18 @@
 QH = 32
 KVH = 8
 EPS = 1e-05
+
+
+def gather_by_bits(x, axis, dim):
+    ways, here = (lax.axis_size(axis), lax.axis_index(axis))
+    grown, reach = (x, 1)
+    while reach < ways:
+        theirs = lax.ppermute(grown, axis, [(d, d ^ reach) for d in range(ways)])
+        mine_first = jnp.concatenate([grown, theirs], axis=dim)
+        theirs_first = jnp.concatenate([theirs, grown], axis=dim)
+        grown = jnp.where(here & reach == 0, mine_first, theirs_first)
+        reach = 2 * reach
+    return grown
 
 
 def passed_along(block, axis, distance):
@@ -35,7 +47,7 @@
     kv_local = keyval.shape[1] // (2 * HD)
     group = QH // KVH
     q_width = kv_local * group * HD
-    flat = lax.all_gather(attn_flat[0, 0], "dp", axis=0, tiled=True)
+    flat = gather_by_bits(attn_flat[0, 0], "dp", 0)
     w_query = flat[: width * q_width].reshape(width, q_width)
     w_out = flat[width * q_width : 2 * width * q_width].reshape(q_width, width)
     query = jnp.dot(normed, w_query, preferred_element_type=jnp.float32).astype(jnp.bfloat16)

time: 865 us -> 735 us (0.85)
  waiting for transfers between devices: 577 us -> 125 us
  blocking collectives: 36.9 us -> 374 us
  local copies, waits for them, and re-layouts: 215 us -> 59.7 us
  other arithmetic: 6.63 us -> 127 us
  matrix products: 11 us -> 24.9 us
    all_gather x1 -> x0, waiting for transfers between devices: 542 us -> none  [shards(): flat = lax.all_gather(attn_flat[0, 0], 'dp', axis=0, tiled=True)]
    all_gather x1, blocking collectives: 17.4 us -> 354 us  [shards(): piece = lax.all_gather(keyval, 'dp', axis=0, tiled=True)]
    slice x3 -> x0, local copies, waits for them, and re-layouts: 210 us -> none  [the longest x2 197 us: shards(): w_out = flat[width * q_width:2 * width * q_width].reshape(q_width, width)]
    ppermute x0 -> x2, waiting for transfers between devices: none -> 90.9 us  [gather_by_bits(): theirs = lax.ppermute(grown, axis, [(d, d ^ reach) for d in range(ways)])]
    unnamed x0 -> x1, other arithmetic: none -> 90 us
    concatenate x0 -> x6, local copies, waits for them, and re-layouts: none -> 55.9 us  [gather_by_bits(): mine_first = jnp.concatenate([grown, theirs], axis=dim)]
    select_n x0 -> x3, other arithmetic: none -> 29.9 us  [gather_by_bits(): grown = jnp.where(here & reach == 0, mine_first, theirs_first)]
    dot_general x1, matrix products: 2.25 us -> 11.1 us  [shards(): partial_value = jnp.dot(mixed, w_out, preferred_element_type=jnp.float32)]
  transfers between devices with their start and end apart: 3 -> 4, of which waited for: 3 -> 3; matrix products, arithmetic and copies ran while one was open for 1% -> 8% of each run, Pallas kernels for 0% -> 0%
where the time goes in v1:
time: 735 us; the launch traced here: 734 us
  blocking collectives  374 us (51%)
  other arithmetic  127 us (17%)
  waiting for transfers between devices  125 us (17%)
  local copies, waits for them, and re-layouts  59.7 us (8%)
  matrix products  24.9 us (3%)
  between operations  14.2 us (2%)
  starting transfers between devices  9.32 us (1%)
    all_gather x1, blocking collectives, shards(): piece = lax.all_gather(keyval, 'dp', axis=0, tiled=True)  354 us
    ppermute x2, waiting for transfers between devices, gather_by_bits(): theirs = lax.ppermute(grown, axis, [(d, d ^ reach) for d in range(ways)])  90.9 us
    unnamed x1, other arithmetic  90 us
    concatenate x6, local copies, waits for them, and re-layouts, gather_by_bits(): mine_first = jnp.concatenate([grown, theirs], axis=dim)  55.9 us
    psum x1, waiting for transfers between devices, shards(): lax.psum(partial_value.astype(jnp.bfloat16), 'mp').astype(jnp.float32)  34.4 us
    select_n x3, other arithmetic, gather_by_bits(): grown = jnp.where(here & reach == 0, mine_first, theirs_first)  29.9 us
    psum x1, blocking collectives, shards(): lax.psum((jnp.where(at_end, squares, 0.0), jnp.where(at_end, product, 0.0...  19.5 us
  transfers between devices with their start and end apart: 4, of which 3 were waited for; matrix products, arithmetic and copies ran while one was open for 8% of the time, Pallas kernels for 0%

profile of v1, /device:TPU:0, one launch (start us, length us, event | category | flops | bytes accessed | tf_op | source)
XLA Modules:
  0.0 733.9 jit_solution(6778951180929668952)
XLA Ops:
  7.2 0.0 all-reduce.3.cloned.1.call-start
  7.2 90.0 %reduce = bf16[2097152]{0:T(1024)(128)(2,1)} reduce(bf16[1,1,2097152]{2,1,0:T(2,128)(2,1)} %param.11, bf16[]{:T(256)} %constant.65), dimensions={0,1}, to_apply=%param.11.reduce_sub_computation | reduce | bytes 8388610 | tf_op args[3]
  97.2 3.0 collective-permute-start
  100.3 90.9 %collective-permute-done = bf16[2097152]{0:T(1024)(128)(2,1)} collective-permute-done((bf16[2097152]{0:T(1024)(128)(2,1)}, bf16[2097152]{0:T(1024)(128)(2,1)}, u32[]{:S(2)}, u32[]{:S(2)}) %collective-permute-start) | collective-permute-done | bytes 4194336 | tf_op jit(solution)/shard_map/ppermute | solution.py:16
  191.2 13.0 %maximum_select_fusion.1 = bf16[4194304]{0:T(1024)(128)(2,1)} fusion(bf16[2097152]{0:T(1024)(128)(2,1)} %collective-permute-done, bf16[2097152]{0:T(1024)(128)(2,1)} %reduce, pred[]{:T(512)S(6)} %eq.69), kind=kLoop, calls=%fused_computation.10 | loop fusion | flops 37748736 | bytes 16777216 | tf_op jit(solution)/shard_map/jit(_where)/select_n | solution.py:19
  204.2 2.8 collective-permute-start.1
  207.0 7.3 concatenate.44
  214.3 7.3 concatenate.53
  221.7 0.0 copy-done.2
  221.7 0.3 fusion.18
  222.0 0.0 copy-done.8
  222.0 2.9 fusion.32
  224.9 354.4 %all_gather.3 = bf16[512,512]{1,0:T(8,128)(2,1)S(1)} all-gather(bf16[128,512]{1,0:T(8,128)(2,1)S(1)} %fusion.32), channel_id=1, replica_groups=mesh['section'=2,'dp'=4,'mp'=4] {'dp'}, dimensions={0}, use_global_device_ids=true | all-gather | bytes 655360 | tf_op jit(solution)/shard_map/all_gather | solution.py:58
  579.3 0.1 reshape.167
  579.4 0.7 fusion.66
  580.1 0.7 copy.22
  580.9 0.0 copy-done.7
  580.9 0.6 fusion.60
  581.5 0.1 select_reduce_fusion
  581.6 0.7 or_and_fusion
  582.2 0.2 fusion.51
  582.5 7.3 concatenate.45
  589.8 7.3 concatenate.54
  597.1 10.5 %maximum_select_fusion = bf16[4096,1024]{1,0:T(8,128)(2,1)} fusion(bf16[2048,1024]{1,0:T(8,128)(2,1)} %concatenate.45, bf16[2048,1024]{1,0:T(8,128)(2,1)} %concatenate.44, pred[]{:T(512)S(6)} %eq.69), kind=kLoop, calls=%fused_computation.9 | loop fusion | flops 37748736 | bytes 16777216 | tf_op jit(solution)/shard_map/jit(_where)/select_n | solution.py:19
  607.6 0.0 copy-done
  607.6 1.1 copy-done.1
  608.7 6.3 maximum_select_fusion.2
  615.0 0.0 collective-permute-done.1
  615.0 13.3 %concatenate.50 = bf16[4096,1024]{1,0:T(8,128)(2,1)} reshape(bf16[4194304]{0:T(1024)(128)(2,1)} %collective-permute-done.1) | data formatting | bytes 16777216 | tf_op jit(solution)/shard_map/concatenate | solution.py:17
  628.3 9.7 %fusion.29 = bf16[128,1024]{1,0:T(8,128)(2,1)S(1)} fusion(bf16[4096,1024]{1,0:T(8,128)(2,1)} %concatenate.50, bf16[4096,1024]{1,0:T(8,128)(2,1)} %maximum_select_fusion, pred[]{:T(512)S(6)} %eq.68, bf16[1,128,4096]{2,1,0:T(8,128)(2,1)S(1)} %copy-done.2, f32[4096]{0:T(1024)S(1)} %bitcast.70, f32[128]{0:T(128)S(1)} %add_rsqrt_fusion), kind=kOutput, calls=%fused_computation.37 | convolution fusion | flops 1113718784 | bytes 18104832 | tf_op jit(solution)/shard_map/dot_general | solution.py:53
  638.0 0.2 reshape.168
  638.2 0.5 fusion.24
  638.7 0.5 fusion.25
  639.2 0.7 fusion.28
  639.9 13.3 %concatenate.57 = bf16[1024,4096]{1,0:T(8,128)(2,1)} reshape(bf16[4194304]{0:T(1024)(128)(2,1)} %collective-permute-done.1) | data formatting | bytes 16777216 | tf_op jit(solution)/shard_map/concatenate | solution.py:17
  653.2 11.1 %fusion.10 = bf16[128,4096]{1,0:T(8,128)(2,1)} fusion(bf16[128,1024]{0,1:T(8,128)(2,1)S(1)} %bitcast.71, bf16[1024,4096]{1,0:T(8,128)(2,1)} %concatenate.57, bf16[1024,4096]{1,0:T(8,128)(2,1)} %maximum_select_fusion.2, pred[]{:T(512)S(6)} %eq.68), kind=kOutput, calls=%fused_computation.15 | convolution fusion | flops 1112014848 | bytes 18087936 | tf_op jit(solution)/shard_map/dot_general | solution.py:87
  664.3 0.0 all-reduce.3.cloned.1.call-update
  664.3 0.2 fusion.59
  664.5 34.4 %all-reduce.3.cloned.1.call-done = bf16[128,4096]{1,0:T(8,128)(2,1)} async-done(((bf16[128,4096]{1,0:T(8,128)(2,1)}), bf16[128,4096]{1,0:T(8,128)(2,1)}) %all-reduce.3.cloned.1.call-update) | async-done | bytes 1048592 | tf_op jit(solution)/shard_map/psum | solution.py:98
  698.9 1.5 fusion.21
  700.4 3.4 collective-permute-start.2
  703.9 0.0 copy-done.3
  703.9 0.6 multiply_reduce_fusion
  704.5 1.3 broadcast_select_fusion
  705.8 19.5 %all-reduce = (f32[2]{0:T(128)S(1)}, f32[2]{0:T(128)S(1)}) all-reduce(f32[2]{0:T(128)S(1)} %get-tuple-element.10, f32[2]{0:T(128)S(1)} %get-tuple-element.9), channel_id=1, replica_groups=mesh['section'=2,'dp'=4,'mp'=4] {'section','dp'}, use_global_device_ids=true, to_apply=%region_8.9 | all-reduce | flops 4 | bytes 32 | tf_op jit(solution)/shard_map/psum | solution.py:104
  725.3 0.7 compare_select_fusion.1
  726.0 0.1 collective-permute-done.2
  726.1 1.0 copy.34
  (19 shorter events, 0.1 us)
Async XLA Ops:
  7.2 691.7 %all-reduce.3.cloned.1.call-start = ((), (), s32[]{:S(2)}) async-start(), calls=%async_computation | async-start | bytes 2097152 | tf_op jit(solution)/shard_map/psum | solution.py:98
  97.2 93.9 %collective-permute-start = (bf16[2097152]{0:T(1024)(128)(2,1)}, bf16[2097152]{0:T(1024)(128)(2,1)}, u32[]{:S(2)}, u32[]{:S(2)}) collective-permute-start(bf16[2097152]{0:T(1024)(128)(2,1)} %reduce), channel_id=1, source_target_pairs={{0,4},{4,0},{8,12},{12,8},{1,5},{5,1},{9,13},{13,9},{2,6},{6,2},{1... | collective-permute-start | bytes 12582920 | tf_op jit(solution)/shard_map/ppermute | solution.py:16
  204.2 17.5 %copy-start.2 = (bf16[1,128,4096]{2,1,0:T(8,128)(2,1)S(1)}, bf16[1,128,4096]{2,1,0:T(8,128)(2,1)}, u32[]{:S(2)}) copy-start(bf16[1,128,4096]{2,1,0:T(8,128)(2,1)} %param.8) | copy-start | bytes 3145732
  204.2 17.8 %copy-start.8 = (f32[1,4096]{1,0:T(1,128)S(1)}, f32[1,4096]{1,0:T(1,128)}, u32[]{:S(2)}) copy-start(f32[1,4096]{1,0:T(1,128)} %param.9) | copy-start | bytes 49156
  204.2 410.8 %collective-permute-start.1 = (bf16[4194304]{0:T(1024)(128)(2,1)}, bf16[4194304]{0:T(1024)(128)(2,1)}, u32[]{:S(2)}, u32[]{:S(2)}) collective-permute-start(bf16[4194304]{0:T(1024)(128)(2,1)} %maximum_select_fusion.1), channel_id=1, source_target_pairs={{0,8},{4,12},{8,0},{12,4},{1,9},{5,13},{9,1},{13,5},{2,10},{6,14},... | collective-permute-start | bytes 25165832 | tf_op jit(solution)/shard_map/ppermute | solution.py:16
  214.3 366.5 %copy-start.7 = (s32[1,4]{1,0:T(1,128)S(1)}, s32[1,4]{1,0:T(1,128)}, u32[]{:S(2)}) copy-start(s32[1,4]{1,0:T(1,128)} %param.14) | copy-start | bytes 52
  597.1 10.5 %copy-start = (bf16[512,4096]{1,0:T(8,128)(2,1)S(1)}, bf16[512,4096]{1,0:T(8,128)(2,1)}, u32[]{:S(2)}) copy-start(bf16[512,4096]{1,0:T(8,128)(2,1)} %concatenate.53) | copy-start | bytes 12582916
  597.1 11.7 %copy-start.1 = (bf16[512,4096]{1,0:T(8,128)(2,1)S(1)}, bf16[512,4096]{1,0:T(8,128)(2,1)}, u32[]{:S(2)}) copy-start(bf16[512,4096]{1,0:T(8,128)(2,1)} %concatenate.54) | copy-start | bytes 12582916
  653.2 50.7 %copy-start.3 = (f32[4096]{0:T(1024)S(1)}, f32[4096]{0:T(1024)}, u32[]{:S(2)}) copy-start(f32[4096]{0:T(1024)} %param.13) | copy-start | bytes 49156
  653.2 50.7 %copy-start.4 = (f32[4096]{0:T(1024)S(1)}, f32[4096]{0:T(1024)}, u32[]{:S(2)}) copy-start(f32[4096]{0:T(1024)} %param.12) | copy-start | bytes 49156
  653.2 72.1 %copy-start.5 = (s32[2]{0:T(128)S(1)}, s32[2]{0:T(128)}, u32[]{:S(2)}) copy-start(s32[2]{0:T(128)} %param.15) | copy-start | bytes 28
  700.4 25.7 %collective-permute-start.2 = (bf16[128,4096]{1,0:T(8,128)(2,1)S(1)}, bf16[128,4096]{1,0:T(8,128)(2,1)S(1)}, u32[]{:S(2)}, u32[]{:S(2)}) collective-permute-start(bf16[128,4096]{1,0:T(8,128)(2,1)S(1)} %fusion.21), channel_id=1, source_target_pairs={{0,16},{1,17},{2,18},{3,19},{4,20},{5,21},{6,22},{7,23},{8,24},{9,... | collective-permute-start | bytes 3145736 | tf_op jit(solution)/shard_map/ppermute | solution.py:27
  725.3 1.8 copy-start.6
Sparse Core Ops, SparseCore 0:
  664.4 34.4 all-reduce.2
